TPU v7x, 256 devices: a whole 4x4x8 slice. The times are simulated.
256 devices in a mesh: ctx: 64 (over x, z_lo, y, core), head: 4 (over z_hi).
Axes of the slice: x: 4, y: 4, z: 8 (z_hi: 4, z_lo: 2; z = z_hi * 2 + z_lo), core: 2. Of those that a mesh axis runs over, the one named last changes fastest.
Arguments:
- query_vecs: bfloat16 [16384, 4096], P('ctx', 'head'), may hold values from -16 to 16
- key_vecs: bfloat16 [16384, 4096], P('ctx', 'head'), may hold values from -16 to 16
- value_vecs: bfloat16 [16384, 4096], P('ctx', 'head'), may hold values from -9 to 9
- out_grad: bfloat16 [16384, 4096], P('ctx', 'head'), may hold values from -9 to 9
- block_mask: int32 [256, 4], P('ctx'), may hold values from -1 to 255, as said below
- norm_gain: float32 [32, 128], P('head'), may hold values from 0.25 to 1.75
Outputs:
- normed: bfloat16 [16384, 4096], P('ctx', 'head')
- query_grad: bfloat16 [16384, 4096], P('ctx', 'head')
- key_grad: bfloat16 [16384, 4096], P('ctx', 'head')
- value_grad: bfloat16 [16384, 4096], P('ctx', 'head')
- gain_grad: float32 [32, 128], P('head')
Inputs may be any that keep to these rules, and one draw needn't show every extreme that they name: `block_mask`: entry 0 of row b is b; every other entry is -1 (no block) or a block index within 2 of b, and the indices of one row are distinct.
All inputs are finite; a program needn't handle non-finite values.
Results may differ from a plain program's by a relative error of at most 0.0073.
Values may be sent and summed in bfloat16 or wider, within the bound.
No kernel may reach another device: no remote copies, remote signals or barrier semaphores. Data moves between devices by JAX's collectives and lax.ppermute only.
A program may use at most 128 MiB of HBM per device.

v0:
```python
import math

import jax
import jax.numpy as jnp
from jax import lax
from jax.sharding import PartitionSpec as P

HEAD_FEATURES = 128
BLOCK = 64
BAND = 2
BLOCKS_DEV = 4
WIDTH = 4096


def shifted(shard, axis, by):
    devices = lax.axis_size(axis)
    pairs = [(i, i + by) for i in range(devices) if 0 <= i + by < devices]
    return lax.ppermute(shard, axis, pairs)


def padded(cells, sides, width):
    for axis, dim in sides:
        count = lax.axis_size(axis)
        ends = count - 1
        head = lax.slice_in_dim(cells, 0, width, axis=dim)
        tail = lax.slice_in_dim(cells, cells.shape[dim] - width, cells.shape[dim], axis=dim)
        cells = jnp.concatenate(
            [
                lax.ppermute(tail, axis, [(i, (i + 1) % count) for i in range(ends)]),
                cells,
                lax.ppermute(head, axis, [((i + 1) % count, i) for i in range(ends)]),
            ],
            axis=dim,
        )
    return cells


def laid_out(parts, dim):
    shape = list(parts.shape[1:])
    shape[dim] *= parts.shape[0]
    return jnp.moveaxis(parts, 0, dim).reshape(shape)


def copy_for_each(shard, axis):
    devices = lax.axis_size(axis)
    return lax.all_to_all(
        jnp.broadcast_to(shard[None], (devices, *shard.shape)), axis, 0, 0, tiled=True
    )


def collect(shard, axis, dim):
    return laid_out(copy_for_each(shard, axis), dim)


def taken_together(shard, axis):
    return copy_for_each(shard, axis).sum(axis=0)


def listing(block_list, offset):
    is_live = block_list >= 0
    slot_index = jnp.where(is_live, block_list - offset, 0)
    return (slot_index, is_live)


def pick_rows(extended, slot_index, heads_here):
    picked = extended[slot_index]
    return picked.reshape(
        slot_index.shape[0], slot_index.shape[1] * BLOCK, heads_here, HEAD_FEATURES
    )


def attend_forward(query_block_list, key_row_vectors, value_row_vectors, is_live):
    factor = HEAD_FEATURES ** (-0.5)
    logit_scores = (
        jnp.einsum(
            "bqhd,bkhd->bhqk", query_block_list, key_row_vectors, preferred_element_type=jnp.float32
        )
        * factor
    )
    columns = jnp.repeat(is_live, BLOCK, axis=1)
    logit_scores = jnp.where(columns[:, None, None, :], logit_scores, -1e30)
    highest = jnp.max(logit_scores, axis=-1, keepdims=True)
    powers = jnp.exp(logit_scores - highest)
    total = jnp.sum(powers, axis=-1, keepdims=True)
    weights = powers / total
    rounded_values = weights.astype(jnp.bfloat16)
    attended = jnp.einsum(
        "bhqk,bkhd->bqhd", rounded_values, value_row_vectors, preferred_element_type=jnp.float32
    )
    log_total = (highest + jnp.log(total))[..., 0]
    return (weights, rounded_values, attended, log_total)


def attend_backward(query_block_list, gradient_block_list, ext_blocks, strand):
    (
        slot_index,
        is_live,
        key_row_vectors,
        value_row_vectors,
        weights,
        rounded_values,
        attended,
        log_total,
    ) = strand
    factor = HEAD_FEATURES ** (-0.5)
    weight_gradient = jnp.einsum(
        "bqhd,bkhd->bhqk",
        gradient_block_list,
        value_row_vectors,
        preferred_element_type=jnp.float32,
    )
    centre = jnp.sum(weights * weight_gradient, axis=-1, keepdims=True)
    score_gradient = (weights * (weight_gradient - centre)).astype(jnp.bfloat16)
    query_contributions = (
        jnp.einsum(
            "bhqk,bkhd->bqhd", score_gradient, key_row_vectors, preferred_element_type=jnp.float32
        )
        * factor
    )
    value_contributions = jnp.einsum(
        "bhqk,bqhd->bkhd", rounded_values, gradient_block_list, preferred_element_type=jnp.float32
    )
    key_contributions = (
        jnp.einsum(
            "bhqk,bqhd->bkhd", score_gradient, query_block_list, preferred_element_type=jnp.float32
        )
        * factor
    )
    slots_total = slot_index.shape[0] * slot_index.shape[1]
    placement = (
        jnp.arange(ext_blocks)[:, None] == slot_index.reshape(slots_total)[None, :]
    ) & is_live.reshape(slots_total)[None, :]
    placement = placement.astype(jnp.float32)
    stacked = jnp.stack([key_contributions, value_contributions]).reshape(2, slots_total, -1)
    spread = jnp.einsum("ns,asr->anr", placement, stacked)
    features = query_block_list.shape[2] * HEAD_FEATURES
    return (query_contributions, spread.reshape(2, ext_blocks * BLOCK, features), centre[..., 0])


def settle_sum(spread, rim_rows, own_rows):
    lower_rim = spread[:, :rim_rows]
    upper_rim = spread[:, rim_rows + own_rows :]
    from_above = shifted(lower_rim.astype(jnp.bfloat16), "ctx", -1).astype(lower_rim.dtype)
    from_below = shifted(upper_rim.astype(jnp.bfloat16), "ctx", 1).astype(upper_rim.dtype)
    middle = spread[:, rim_rows : rim_rows + own_rows]
    middle = middle.at[:, :rim_rows].add(from_below)
    return middle.at[:, own_rows - rim_rows :].add(from_above)


def body(query_vecs, key_vecs, value_vecs, out_grad, block_mask, norm_gain):
    own_rows = query_vecs.shape[0]
    features = query_vecs.shape[1]
    heads_here = features // HEAD_FEATURES
    rim_rows = BAND * BLOCK
    ext_blocks = BLOCKS_DEV + 2 * BAND
    devices = lax.axis_size("ctx")
    position = lax.axis_index("ctx")
    all_blocks = BLOCKS_DEV * devices
    banded = padded(jnp.stack([key_vecs, value_vecs]), (("ctx", 1),), rim_rows)
    key_ext = banded[0].reshape(ext_blocks, BLOCK, features)
    value_ext = banded[1].reshape(ext_blocks, BLOCK, features)
    full_mask = collect(block_mask, "ctx", 0)
    first_row = all_blocks - (position + 1) * BLOCKS_DEV
    mirror_rows = lax.dynamic_slice_in_dim(full_mask, first_row, BLOCKS_DEV, 0)[::-1]
    reflected = jnp.where(mirror_rows >= 0, all_blocks - 1 - mirror_rows, -1)
    offset = position * BLOCKS_DEV - BAND
    query_block_list = query_vecs.reshape(BLOCKS_DEV, BLOCK, heads_here, HEAD_FEATURES)
    strands = []
    for block_list in (block_mask, reflected):
        slot_index, is_live = listing(block_list, offset)
        key_row_vectors = pick_rows(key_ext, slot_index, heads_here)
        value_row_vectors = pick_rows(value_ext, slot_index, heads_here)
        weights, rounded_values, attended, log_total = attend_forward(
            query_block_list, key_row_vectors, value_row_vectors, is_live
        )
        strands.append(
            (
                slot_index,
                is_live,
                key_row_vectors,
                value_row_vectors,
                weights,
                rounded_values,
                attended,
                log_total,
            )
        )
    mixed_sum = (strands[0][6] + strands[1][6]).reshape(own_rows, features)
    squares = taken_together(jnp.sum(mixed_sum * mixed_sum, axis=1), "head")
    rms_root = jnp.sqrt(squares / WIDTH + 1e-06)[:, None]
    flat_gain = norm_gain.reshape(features)
    normed = (flat_gain * mixed_sum / rms_root).astype(jnp.bfloat16)
    grad_values = out_grad.astype(jnp.float32)
    scaled_grad = flat_gain * grad_values
    inner_sum = taken_together(jnp.sum(scaled_grad * mixed_sum, axis=1), "head")[:, None] / WIDTH
    mixed_grad = (
        scaled_grad / rms_root - mixed_sum * inner_sum / (rms_root * rms_root * rms_root)
    ).astype(jnp.bfloat16)
    gain_part = jnp.sum(grad_values * mixed_sum / rms_root, axis=0).reshape(
        heads_here, HEAD_FEATURES
    )
    gain_grad = taken_together(gain_part, "ctx") / math.sqrt(own_rows * devices)
    gradient_block_list = mixed_grad.reshape(BLOCKS_DEV, BLOCK, heads_here, HEAD_FEATURES)
    query_one, spread_one, centre_one = attend_backward(
        query_block_list, gradient_block_list, ext_blocks, strands[0]
    )
    query_two, spread_two, centre_two = attend_backward(
        query_block_list, gradient_block_list, ext_blocks, strands[1]
    )
    settled = settle_sum(spread_one + spread_two, rim_rows, own_rows)
    query_grad = (query_one + query_two).reshape(own_rows, features).astype(jnp.bfloat16)
    key_grad = settled[0].astype(jnp.bfloat16)
    value_grad = settled[1].astype(jnp.bfloat16)
    return (normed, query_grad, key_grad, value_grad, gain_grad)


def solution(mesh):
    return jax.shard_map(
        body,
        mesh=mesh,
        in_specs=(
            P("ctx", "head"),
            P("ctx", "head"),
            P("ctx", "head"),
            P("ctx", "head"),
            P("ctx", None),
            P("head", None),
        ),
        out_specs=(
            P("ctx", "head"),
            P("ctx", "head"),
            P("ctx", "head"),
            P("ctx", "head"),
            P("head", None),
        ),
        check_vma=False,
    )
```

profile of v0, /device:TPU:6, one launch (start us, length us, event | category | flops | bytes accessed | tf_op | source)
XLA Modules:
  0.0 174.7 jit_solution(11538806473828333539)
XLA Ops:
  2.1 9.5 %all-to-all-start = ((s32[64,4,4]{2,1,0:T(4,128)}), s32[64,4,4]{2,1,0:T(4,128)S(1)}, u32[]{:S(2)}, u32[]{:S(2)}) async-start(s32[64,4,4]{2,1,0:T(4,128)} %broadcast_in_dim.84), calls=%async_computation | async-start | bytes 262144 | tf_op jit(solution)/shard_map/all_to_all | solution.py:46
  15.0 6.5 %collective-permute-start.1 = (bf16[2,128,1024]{2,1,0:T(8,128)(2,1)S(1)}, bf16[2,128,1024]{2,1,0:T(8,128)(2,1)}, u32[]{:S(2)}, u32[]{:S(2)}) collective-permute-start(bf16[2,128,1024]{2,1,0:T(8,128)(2,1)S(1)} %get-tuple-element.44), channel_id=1, source_target_pairs={{4,0},{8,4},{12,8},{16,12},{20,16},{24,20},{28,24},{32,28},{36,32}... | collective-permute-start | bytes 1572872 | tf_op jit(solution)/shard_map/ppermute | solution.py:31
  22.3 4.3 %collective-permute-done = bf16[2,128,1024]{2,1,0:T(8,128)(2,1)} collective-permute-done((bf16[2,128,1024]{2,1,0:T(8,128)(2,1)S(1)}, bf16[2,128,1024]{2,1,0:T(8,128)(2,1)}, u32[]{:S(2)}, u32[]{:S(2)}) %collective-permute-start) | collective-permute-done | bytes 524320 | tf_op jit(solution)/shard_map/ppermute | solution.py:29
  53.7 7.6 %all-to-all-start.1 = ((f32[4,1,256]{2,1,0:T(1,128)}), f32[4,1,256]{2,1,0:T(1,128)S(1)}, u32[]{:S(2)}, u32[]{:S(2)}) async-start(f32[4,1,256]{2,1,0:T(1,128)} %broadcast_in_dim.91), calls=%async_computation.1 | async-start | bytes 8192 | tf_op jit(solution)/shard_map/all_to_all | solution.py:46
  61.3 2.8 %copy.69 = f32[4,64,8,128]{3,2,1,0:T(8,128)} copy(f32[4,64,8,128]{3,1,2,0:T(8,128)} %get-tuple-element.52) | data formatting | bytes 2097152 | tf_op jit(solution)/shard_map/add | solution.py:188
  64.1 4.9 %all-to-all-done.1 = f32[4,1,256]{2,1,0:T(1,128)S(1)} async-done(((f32[4,1,256]{2,1,0:T(1,128)}), f32[4,1,256]{2,1,0:T(1,128)S(1)}, u32[]{:S(2)}, u32[]{:S(2)}) %all-to-all-start.1) | async-done | bytes 4128 | tf_op jit(solution)/shard_map/all_to_all | solution.py:46
  71.2 3.2 %all-to-all-start.2 = ((f32[4,1,256]{2,1,0:T(1,128)}), f32[4,1,256]{2,1,0:T(1,128)S(1)}, u32[]{:S(2)}, u32[]{:S(2)}) async-start(f32[4,1,256]{2,1,0:T(1,128)} %broadcast_in_dim.92), calls=%async_computation.2 | async-start | bytes 8192 | tf_op jit(solution)/shard_map/all_to_all | solution.py:46
  74.8 7.3 %all-to-all-done.2 = f32[4,1,256]{2,1,0:T(1,128)S(1)} async-done(((f32[4,1,256]{2,1,0:T(1,128)}), f32[4,1,256]{2,1,0:T(1,128)S(1)}, u32[]{:S(2)}, u32[]{:S(2)}) %all-to-all-start.2) | async-done | bytes 4128 | tf_op jit(solution)/shard_map/all_to_all | solution.py:46
  82.8 7.2 %all-to-all-start.3 = ((f32[64,8,128]{2,1,0:T(8,128)}), f32[64,8,128]{2,1,0:T(8,128)S(1)}, u32[]{:S(2)}, u32[]{:S(2)}) async-start(f32[64,8,128]{2,1,0:T(8,128)} %broadcast_in_dim.94), calls=%async_computation.3 | async-start | bytes 524288 | tf_op jit(solution)/shard_map/all_to_all | solution.py:46
  92.7 3.8 %multiply_reduce_fusion = (f32[4,8,64]{2,1,0:T(8,128)S(1)}, f32[4,8,64,256]{3,2,1,0:T(8,128)}) fusion(f32[4,8,64,256]{3,2,1,0:T(8,128)S(1)} %copy-done.12, f32[4,8,64]{2,1,0:T(8,128)S(1)} %get-tuple-element.47, bf16[4,256,8,128]{3,2,1,0:T(8,128)(2,1)} %bitcast.133, bf16[4,64,8,128]{3,2,1,0:T(8,128)(2,1)S(1)} %bitcast.141), kind=kOutput, calls=%fused_computation.29 | convolution fusion | flops 135788544 | bytes 6832128 | tf_op jit(solution)/shard_map/bqhd,bkhd->bhqk/dot_general | solution.py:106
  104.0 4.3 %copy.86 = bf16[4,256,8,128]{3,2,1,0:T(8,128)(2,1)} copy(bf16[4,256,8,128]{1,3,2,0:T(8,128)(2,1)} %convolution_bitcast_fusion) | data formatting | bytes 4194304 | tf_op jit(solution)/shard_map/bhqk,bqhd->bkhd/transpose | solution.py:120
  108.3 3.2 %stack.34 = bf16[1,16,65536]{2,1,0:T(8,128)(2,1)} reshape(bf16[4,256,8,128]{3,2,1,0:T(8,128)(2,1)} %copy.86) | data formatting | bytes 4194304 | tf_op jit(solution)/shard_map/stack | solution.py:134
  111.5 4.3 %copy.82 = bf16[4,256,8,128]{3,2,1,0:T(8,128)(2,1)} copy(bf16[4,256,8,128]{1,3,2,0:T(8,128)(2,1)} %convolution_bitcast_fusion.1) | data formatting | bytes 4194304 | tf_op jit(solution)/shard_map/bhqk,bqhd->bkhd/transpose | solution.py:120
  115.8 3.1 %stack.31 = bf16[1,16,65536]{2,1,0:T(8,128)(2,1)} reshape(bf16[4,256,8,128]{3,2,1,0:T(8,128)(2,1)} %copy.82) | data formatting | bytes 4194304 | tf_op jit(solution)/shard_map/stack | solution.py:134
  123.3 2.7 %copy.80 = bf16[4,256,8,128]{3,2,1,0:T(8,128)(2,1)} copy(bf16[4,256,8,128]{3,1,2,0:T(8,128)(2,1)S(1)} %multiply_bitcast_fusion.1) | data formatting | bytes 4194304 | tf_op jit(solution)/shard_map/mul | solution.py:124
  126.0 3.1 %stack.30 = bf16[1,16,65536]{2,1,0:T(8,128)(2,1)} reshape(bf16[4,256,8,128]{3,2,1,0:T(8,128)(2,1)} %copy.80) | data formatting | bytes 4194304 | tf_op jit(solution)/shard_map/stack | solution.py:134
  132.8 2.7 %copy.84 = bf16[4,256,8,128]{3,2,1,0:T(8,128)(2,1)} copy(bf16[4,256,8,128]{3,1,2,0:T(8,128)(2,1)S(1)} %multiply_bitcast_fusion) | data formatting | bytes 4194304 | tf_op jit(solution)/shard_map/mul | solution.py:124
  135.4 3.1 %stack.33 = bf16[1,16,65536]{2,1,0:T(8,128)(2,1)} reshape(bf16[4,256,8,128]{3,2,1,0:T(8,128)(2,1)} %copy.84) | data formatting | bytes 4194304 | tf_op jit(solution)/shard_map/stack | solution.py:134
  138.6 3.1 %fusion.3 = f32[2,65536,8]{1,2,0:T(8,128)S(1)} fusion(bf16[1,16,65536]{2,1,0:T(8,128)(2,1)} %stack.31, bf16[1,16,65536]{2,1,0:T(8,128)(2,1)} %stack.30, s32[16]{0:T(128)S(1)} %eq.31, pred[16]{0:T(512)(128)(4,1)S(1)} %and.27), kind=kOutput, calls=%fused_computation.8 | convolution fusion | flops 35651840 | bytes 8388688 | tf_op jit(solution)/shard_map/ns,asr->anr/dot_general | solution.py:135
  142.0 2.9 %fusion.2 = f32[2,8,65536]{2,1,0:T(8,128)} fusion(f32[2,65536,8]{1,2,0:T(8,128)S(1)} %fusion.3, bf16[1,16,65536]{2,1,0:T(8,128)(2,1)S(1)} %copy-done.6, bf16[1,16,65536]{2,1,0:T(8,128)(2,1)S(1)} %copy-done.7, s32[16]{0:T(128)S(1)} %eq.35, pred[16]{0:T(512)(128)(4,1)S(1)} %and.30), kind=kOutput, calls=%fused_computation.7 | convolution fusion | flops 36700416 | bytes 12582992 | tf_op jit(solution)/shard_map/ns,asr->anr/dot_general | solution.py:135
  144.9 3.9 %add.73 = f32[2,512,1024]{2,1,0:T(8,128)} reshape(f32[2,8,65536]{2,1,0:T(8,128)} %fusion.2) | data formatting | bytes 8388608 | tf_op jit(solution)/shard_map/add | solution.py:210
  148.9 2.6 %convert.8 = bf16[2,512,1024]{2,1,0:T(8,128)(2,1)S(1)} convert(f32[2,512,1024]{2,1,0:T(8,128)} %add.73) | non-fusion elementwise | flops 1048576 | bytes 6291456 | tf_op jit(solution)/shard_map/convert.3
  152.5 5.5 %collective-permute-start.3 = (bf16[2,128,1024]{2,1,0:T(8,128)(2,1)}, bf16[2,128,1024]{2,1,0:T(8,128)(2,1)S(1)}, u32[]{:S(2)}, u32[]{:S(2)}) collective-permute-start(bf16[2,128,1024]{2,1,0:T(8,128)(2,1)} %get-tuple-element.35), channel_id=1, source_target_pairs={{4,0},{8,4},{12,8},{16,12},{20,16},{24,20},{28,24},{32,28},{36,32}... | collective-permute-start | bytes 1572872 | tf_op jit(solution)/shard_map/ppermute | solution.py:18
  163.0 8.9 %collective-permute-done.2 = bf16[2,128,1024]{2,1,0:T(8,128)(2,1)S(1)} collective-permute-done((bf16[2,128,1024]{2,1,0:T(8,128)(2,1)}, bf16[2,128,1024]{2,1,0:T(8,128)(2,1)S(1)}, u32[]{:S(2)}, u32[]{:S(2)}) %collective-permute-start.2) | collective-permute-done | bytes 524320 | tf_op jit(solution)/shard_map/ppermute | solution.py:18
  (122 shorter events, 62.9 us)
Async XLA Ops:
  0.6 20.9 %copy-start.22 = (s32[4,4]{1,0:T(4,128)S(1)}, s32[4,4]{1,0:T(4,128)}, u32[]{:S(2)}) copy-start(s32[4,4]{1,0:T(4,128)} %param.14) | copy-start | bytes 196
  0.6 27.6 %copy-start.20 = (bf16[256,1024]{1,0:T(8,128)(2,1)S(1)}, bf16[256,1024]{1,0:T(8,128)(2,1)}, u32[]{:S(2)}) copy-start(bf16[256,1024]{1,0:T(8,128)(2,1)} %param.12) | copy-start | bytes 1572868
  0.7 27.6 %copy-start.19 = (bf16[256,1024]{1,0:T(8,128)(2,1)S(1)}, bf16[256,1024]{1,0:T(8,128)(2,1)}, u32[]{:S(2)}) copy-start(bf16[256,1024]{1,0:T(8,128)(2,1)} %param.11) | copy-start | bytes 1572868
  0.7 21.2 %copy-start.21 = (bf16[256,1024]{1,0:T(8,128)(2,1)S(1)}, bf16[256,1024]{1,0:T(8,128)(2,1)}, u32[]{:S(2)}) copy-start(bf16[256,1024]{1,0:T(8,128)(2,1)} %param.10) | copy-start | bytes 1572868
  2.1 19.8 %all-to-all-start = ((s32[64,4,4]{2,1,0:T(4,128)}), s32[64,4,4]{2,1,0:T(4,128)S(1)}, u32[]{:S(2)}, u32[]{:S(2)}) async-start(s32[64,4,4]{2,1,0:T(4,128)} %broadcast_in_dim.84), calls=%async_computation | async-start | bytes 262144 | tf_op jit(solution)/shard_map/all_to_all | solution.py:46
  12.9 13.6 %collective-permute-start = (bf16[2,128,1024]{2,1,0:T(8,128)(2,1)S(1)}, bf16[2,128,1024]{2,1,0:T(8,128)(2,1)}, u32[]{:S(2)}, u32[]{:S(2)}) collective-permute-start(bf16[2,128,1024]{2,1,0:T(8,128)(2,1)S(1)} %get-tuple-element.43), channel_id=1, source_target_pairs={{0,4},{4,8},{8,12},{12,16},{16,20},{20,24},{24,28},{28,32},{32,36}... | collective-permute-start | bytes 1572872 | tf_op jit(solution)/shard_map/ppermute | solution.py:29
  15.0 13.2 %collective-permute-start.1 = (bf16[2,128,1024]{2,1,0:T(8,128)(2,1)S(1)}, bf16[2,128,1024]{2,1,0:T(8,128)(2,1)}, u32[]{:S(2)}, u32[]{:S(2)}) collective-permute-start(bf16[2,128,1024]{2,1,0:T(8,128)(2,1)S(1)} %get-tuple-element.44), channel_id=1, source_target_pairs={{4,0},{8,4},{12,8},{16,12},{20,16},{24,20},{28,24},{32,28},{36,32}... | collective-permute-start | bytes 1572872 | tf_op jit(solution)/shard_map/ppermute | solution.py:31
  40.2 9.7 %copy-start.17 = (bf16[128,8,8,128]{3,2,1,0:T(8,128)(2,1)}, bf16[128,8,8,128]{3,2,1,0:T(8,128)(2,1)S(1)}, u32[]{:S(2)}) copy-start(bf16[128,8,8,128]{3,2,1,0:T(8,128)(2,1)S(1)} %copy.93) | copy-start | bytes 6291460
  40.3 3.1 %copy-start.9 = (bf16[16,64,1024]{2,1,0:T(8,128)(2,1)S(1)}, bf16[16,64,1024]{2,1,0:T(8,128)(2,1)}, u32[]{:S(2)}) copy-start(bf16[16,64,1024]{2,1,0:T(8,128)(2,1)} %gather_fusion.1) | copy-start | bytes 6291460
  40.9 10.1 %copy-start.13 = (bf16[128,8,8,128]{3,2,1,0:T(8,128)(2,1)}, bf16[128,8,8,128]{3,2,1,0:T(8,128)(2,1)S(1)}, u32[]{:S(2)}) copy-start(bf16[128,8,8,128]{3,2,1,0:T(8,128)(2,1)S(1)} %copy.91) | copy-start | bytes 6291460
  53.0 16.0 %copy-start.18 = (bf16[256,1024]{1,0:T(8,128)(2,1)S(1)}, bf16[256,1024]{1,0:T(8,128)(2,1)}, u32[]{:S(2)}) copy-start(bf16[256,1024]{1,0:T(8,128)(2,1)} %param.13) | copy-start | bytes 1572868
  53.0 16.0 %copy-start.23 = (f32[8,128]{1,0:T(8,128)S(1)}, f32[8,128]{1,0:T(8,128)}, u32[]{:S(2)}) copy-start(f32[8,128]{1,0:T(8,128)} %param.15) | copy-start | bytes 12292
  53.7 15.3 %all-to-all-start.1 = ((f32[4,1,256]{2,1,0:T(1,128)}), f32[4,1,256]{2,1,0:T(1,128)S(1)}, u32[]{:S(2)}, u32[]{:S(2)}) async-start(f32[4,1,256]{2,1,0:T(1,128)} %broadcast_in_dim.91), calls=%async_computation.1 | async-start | bytes 8192 | tf_op jit(solution)/shard_map/all_to_all | solution.py:46
  71.2 10.9 %all-to-all-start.2 = ((f32[4,1,256]{2,1,0:T(1,128)}), f32[4,1,256]{2,1,0:T(1,128)S(1)}, u32[]{:S(2)}, u32[]{:S(2)}) async-start(f32[4,1,256]{2,1,0:T(1,128)} %broadcast_in_dim.92), calls=%async_computation.2 | async-start | bytes 8192 | tf_op jit(solution)/shard_map/all_to_all | solution.py:46
  82.8 79.5 %all-to-all-start.3 = ((f32[64,8,128]{2,1,0:T(8,128)}), f32[64,8,128]{2,1,0:T(8,128)S(1)}, u32[]{:S(2)}, u32[]{:S(2)}) async-start(f32[64,8,128]{2,1,0:T(8,128)} %broadcast_in_dim.94), calls=%async_computation.3 | async-start | bytes 524288 | tf_op jit(solution)/shard_map/all_to_all | solution.py:46
  90.0 2.7 %copy-start.12 = (f32[4,8,64,256]{3,2,1,0:T(8,128)S(1)}, f32[4,8,64,256]{3,2,1,0:T(8,128)}, u32[]{:S(2)}) copy-start(f32[4,8,64,256]{3,2,1,0:T(8,128)} %copy-done.11) | copy-start | bytes 6291460
  96.5 3.0 %copy-start.16 = (f32[4,8,64,256]{3,2,1,0:T(8,128)S(1)}, f32[4,8,64,256]{3,2,1,0:T(8,128)}, u32[]{:S(2)}) copy-start(f32[4,8,64,256]{3,2,1,0:T(8,128)} %copy-done.15) | copy-start | bytes 6291460
  138.6 3.1 %copy-start.6 = (bf16[1,16,65536]{2,1,0:T(8,128)(2,1)S(1)}, bf16[1,16,65536]{2,1,0:T(8,128)(2,1)}, u32[]{:S(2)}) copy-start(bf16[1,16,65536]{2,1,0:T(8,128)(2,1)} %stack.34) | copy-start | bytes 6291460
  138.6 3.5 %copy-start.7 = (bf16[1,16,65536]{2,1,0:T(8,128)(2,1)S(1)}, bf16[1,16,65536]{2,1,0:T(8,128)(2,1)}, u32[]{:S(2)}) copy-start(bf16[1,16,65536]{2,1,0:T(8,128)(2,1)} %stack.33) | copy-start | bytes 6291460
  148.9 11.2 %copy-start.5 = (bf16[4,8,64,256]{3,2,1,0:T(8,128)(2,1)S(1)}, bf16[4,8,64,256]{3,2,1,0:T(8,128)(2,1)}, u32[]{:S(2)}) copy-start(bf16[4,8,64,256]{3,2,1,0:T(8,128)(2,1)} %copy-done.4) | copy-start | bytes 3145732
  151.5 8.6 %copy-start.1 = (bf16[128,8,8,128]{3,2,1,0:T(8,128)(2,1)S(1)}, bf16[128,8,8,128]{3,2,1,0:T(8,128)(2,1)}, u32[]{:S(2)}) copy-start(bf16[128,8,8,128]{3,2,1,0:T(8,128)(2,1)} %copy-done) | copy-start | bytes 6291460
  152.5 20.7 %collective-permute-start.3 = (bf16[2,128,1024]{2,1,0:T(8,128)(2,1)}, bf16[2,128,1024]{2,1,0:T(8,128)(2,1)S(1)}, u32[]{:S(2)}, u32[]{:S(2)}) collective-permute-start(bf16[2,128,1024]{2,1,0:T(8,128)(2,1)} %get-tuple-element.35), channel_id=1, source_target_pairs={{4,0},{8,4},{12,8},{16,12},{20,16},{24,20},{28,24},{32,28},{36,32}... | collective-permute-start | bytes 1572872 | tf_op jit(solution)/shard_map/ppermute | solution.py:18
  158.0 13.8 %collective-permute-start.2 = (bf16[2,128,1024]{2,1,0:T(8,128)(2,1)}, bf16[2,128,1024]{2,1,0:T(8,128)(2,1)S(1)}, u32[]{:S(2)}, u32[]{:S(2)}) collective-permute-start(bf16[2,128,1024]{2,1,0:T(8,128)(2,1)} %get-tuple-element.36), channel_id=1, source_target_pairs={{0,4},{4,8},{8,12},{12,16},{16,20},{20,24},{24,28},{28,32},{32,36}... | collective-permute-start | bytes 1572872 | tf_op jit(solution)/shard_map/ppermute | solution.py:18
  161.0 10.8 %slice-start = ((f32[2,512,1024]{2,1,0:T(8,128)}), f32[2,256,1024]{2,1,0:T(8,128)S(1)}, s32[]{:S(2)}) async-start(f32[2,512,1024]{2,1,0:T(8,128)} %add.73), calls=%async_computation.4 | async-start | bytes 4194304 | tf_op jit(solution)/shard_map/slice | solution.py:145
  (9 other events, 14.9 us)
where the time goes:
time: 176 us; the launch traced here: 175 us
  local copies, waits for them, and re-layouts  60.4 us (34%)
  starting transfers between devices  43.6 us (25%)
  waiting for transfers between devices  27.1 us (15%)
  matrix products  23.3 us (13%)
  other arithmetic  19.1 us (11%)
    all_to_all x4, starting transfers between devices, copy_for_each(): lax.all_to_all(jnp.broadcast_to(shard[None], (devices, *shard.shape)), ax...  27.5 us
    another operation x4, local copies, waits for them, and re-layouts, attend_backward(): jnp.stack([key_contributions, value_contributions])  12.5 us
    all_to_all x4, waiting for transfers between devices, copy_for_each(): lax.all_to_all(jnp.broadcast_to(shard[None], (devices, *shard.shape)), ax...  12.3 us
    unnamed x55, local copies, waits for them, and re-layouts  12.1 us
    ppermute x2, waiting for transfers between devices, shifted(): return lax.ppermute(shard, axis, pairs)  8.89 us
    transpose x2, local copies, waits for them, and re-layouts, attend_backward(): jnp.einsum('bhqk,bqhd->bkhd', rounded_values, gradient_block_list, prefer...  8.65 us
    gather x4, local copies, waits for them, and re-layouts, pick_rows(): picked = extended[slot_index]  8.1 us
    ppermute x2, starting transfers between devices, shifted(): return lax.ppermute(shard, axis, pairs)  7.52 us
  transfers between devices with their start and end apart: 8, of which 5 were waited for; matrix products, arithmetic and copies ran while one was open for 40% of the time, Pallas kernels for 0%

commit v1 on v0

v1 whole, which is shorter than its diff:
```python
import functools
import math

import jax
import jax.numpy as jnp
from jax import lax
from jax.experimental import pallas as pl
from jax.experimental.pallas import tpu as pltpu
from jax.sharding import PartitionSpec as P

HEAD_FEATURES = 128
BLOCK = 64
BAND = 2
BLOCKS_DEV = 4
SLOTS = 4
WIDTH = 4096
PAIR = 2 * BLOCK
TILE = 6
FACTOR = HEAD_FEATURES ** (-0.5)
FACTOR2 = FACTOR * math.log2(math.e)
NT = (((1,), (1,)), ((), ()))
NN = (((1,), (0,)), ((), ()))
TN = (((0,), (0,)), ((), ()))
F32 = jnp.float32
BF16 = jnp.bfloat16
VM = pl.BlockSpec(memory_space=pltpu.VMEM)
SM = pl.BlockSpec(memory_space=pltpu.SMEM)


def dot(a, b, dims):
    return lax.dot_general(a, b, dims, preferred_element_type=F32)


def lanes(head):
    return pl.ds(pl.multiple_of(head * HEAD_FEATURES, HEAD_FEATURES), HEAD_FEATURES)


def list_bias(mask_ref, mirror_ref, first, all_blocks):
    result = []
    for strand in range(2):
        rows = []
        for b in range(BLOCKS_DEV):
            row = {}
            for offset in range(-BAND, BAND + 1):
                target = first + b + offset
                hit = None
                for n in range(SLOTS):
                    if strand == 0:
                        entry = mask_ref[b, n]
                        same = (entry >= 0) & (entry == target)
                    else:
                        entry = mirror_ref[BLOCKS_DEV - 1 - b, n]
                        same = (entry >= 0) & (all_blocks - 1 - entry == target)
                    hit = same if hit is None else hit | same
                row[offset] = jnp.where(hit, 0.0, -1e30).astype(F32)
            rows.append(row)
        result.append(rows)
    return result


def pair_bias(bias, strand, pair):
    left = lax.broadcasted_iota(jnp.int32, (1, 1, PAIR), 2) < BLOCK
    rows = []
    for j in range(TILE):
        scalars = []
        for b in range(2):
            offset = j - BAND - b
            inside = -BAND <= offset <= BAND
            scalars.append(bias[strand][2 * pair + b][offset] if inside else -1e30)
        rows.append(jnp.where(left, scalars[0], scalars[1]).astype(F32))
    return jnp.concatenate(rows, axis=0)


def pair_tiles(own, low, high):
    shape = (TILE, BLOCK, PAIR)
    first = jnp.concatenate([low, own[:, :PAIR]], axis=0).reshape(shape)
    second = jnp.concatenate([own[:, PAIR:], high], axis=0).reshape(shape)
    return first, second


def scores(query, key_own, key_low, key_high):
    own = dot(key_own, query, NT)
    low = dot(key_low, query[:PAIR], NT)
    high = dot(key_high, query[PAIR:], NT)
    return pair_tiles(own, low, high)


def forward_kernel(
    mask_ref, mirror_ref, q_ref, k_ref, v_ref, low_ref, high_ref, g_ref, gain_ref,
    mixed_ref, rows_ref, stats_ref, bias_ref, square_ref, inner_ref,
):
    heads = q_ref.shape[1] // HEAD_FEATURES
    devices = lax.axis_size("ctx")
    first = lax.axis_index("ctx") * BLOCKS_DEV
    bias = list_bias(mask_ref, mirror_ref, first, devices * BLOCKS_DEV)
    for strand in range(2):
        for pair in range(2):
            bias_ref[strand, pair] = pair_bias(bias, strand, pair)
    square_ref[...] = jnp.zeros_like(square_ref)
    inner_ref[...] = jnp.zeros_like(inner_ref)

    @pl.loop(0, heads)
    def _(head):
        at = lanes(head)
        query = q_ref[:, at]
        tiles = scores(query, k_ref[:, at], low_ref[0, :, at], high_ref[0, :, at])
        gain = gain_ref[pl.ds(head, 1), :]
        for pair in range(2):
            x = tiles[pair] * FACTOR2
            peak = jnp.max(x, axis=1, keepdims=True)
            p = jnp.exp2(x - peak)
            mass = jnp.sum(p, axis=1, keepdims=True)
            parts = []
            for strand in range(2):
                shifted = peak + bias_ref[strand, pair]
                top = jnp.max(shifted, axis=0, keepdims=True)
                f = jnp.exp2(shifted - top)
                total = jnp.sum(f * mass, axis=0, keepdims=True)
                parts.append(f / total)
            both = parts[0] + parts[1]
            for i, part in enumerate((peak, parts[0], parts[1])):
                rows_ref[head, pair, i] = part[:, 0, :]
            w = (p * both).astype(BF16).reshape(TILE * BLOCK, PAIR)
            if pair == 0:
                v = jnp.concatenate([low_ref[1, :, at], v_ref[:, at]], axis=0)
            else:
                v = jnp.concatenate([v_ref[:, at], high_ref[1, :, at]], axis=0)
            mixed = dot(w, v, TN)
            here = slice(pair * PAIR, (pair + 1) * PAIR)
            mixed_ref[here, at] = mixed
            square_ref[here] += mixed * mixed
            inner_ref[here] += gain * g_ref[here, at].astype(F32) * mixed

    for pair in range(2):
        here = slice(pair * PAIR, (pair + 1) * PAIR)
        for i, ref in enumerate((square_ref, inner_ref)):
            stats_ref[i : i + 1, here] = jnp.sum(ref[here].T, axis=0, keepdims=True)


def backward_kernel(
    stats_ref, q_ref, k_ref, v_ref, low_ref, high_ref, g_ref, gain_ref, mixed_ref, rows_ref,
    normed_ref, dq_ref, own_ref, to_low_ref, to_high_ref, gain_part_ref, one_ref, two_ref,
):
    heads = q_ref.shape[1] // HEAD_FEATURES
    stats = jnp.sum(stats_ref[...], axis=0)
    root = jnp.sqrt(stats[0:1] / WIDTH + 1e-06)
    inverse = 1.0 / root
    slope = (stats[1:2] / WIDTH) * inverse * inverse * inverse
    for pair in range(2):
        here = slice(pair * PAIR, (pair + 1) * PAIR)
        one_ref[here] = jnp.broadcast_to(inverse[:, here], (PAIR, PAIR)).T
        two_ref[here] = jnp.broadcast_to(slope[:, here], (PAIR, PAIR)).T

    @pl.loop(0, heads)
    def _(head):
        at = lanes(head)
        gain = gain_ref[pl.ds(head, 1), :]
        mixed = mixed_ref[:, at]
        raw = g_ref[:, at].astype(F32)
        unit = mixed * one_ref[...]
        normed_ref[:, at] = (gain * unit).astype(BF16)
        gain_part_ref[pl.ds(head, 1), :] = jnp.sum(raw * unit, axis=0, keepdims=True)
        grad = (gain * raw * one_ref[...] - mixed * two_ref[...]).astype(BF16)
        query = q_ref[:, at]
        key = k_ref[:, at]
        tiles = scores(query, key, low_ref[0, :, at], high_ref[0, :, at])
        slopes = scores(grad, v_ref[:, at], low_ref[1, :, at], high_ref[1, :, at])
        ws, ds = [], []
        for pair in range(2):
            peak, f0, f1 = (rows_ref[head, pair, i][:, None, :] for i in range(3))
            p = jnp.exp2(tiles[pair] * FACTOR2 - peak)
            both = f0 + f1
            slope = slopes[pair]
            mass = jnp.sum(p * slope, axis=1, keepdims=True)
            c0 = jnp.sum(f0 * mass, axis=0, keepdims=True)
            c1 = jnp.sum(f1 * mass, axis=0, keepdims=True)
            shape = (TILE * BLOCK, PAIR)
            ws.append((p * both).astype(BF16).reshape(shape))
            ds.append((p * (both * slope - (f0 * c0 + f1 * c1))).astype(BF16).reshape(shape))
        w_own = jnp.concatenate([ws[0][PAIR:], ws[1][: 2 * PAIR]], axis=1)
        d_own = jnp.concatenate([ds[0][PAIR:], ds[1][: 2 * PAIR]], axis=1)
        own_ref[0, :, at] = dot(d_own, query, NN) * FACTOR
        own_ref[1, :, at] = dot(w_own, grad, NN)
        to_low_ref[0, :, at] = (dot(ds[0][:PAIR], query[:PAIR], NN) * FACTOR).astype(BF16)
        to_low_ref[1, :, at] = dot(ws[0][:PAIR], grad[:PAIR], NN).astype(BF16)
        to_high_ref[0, :, at] = (dot(ds[1][2 * PAIR :], query[PAIR:], NN) * FACTOR).astype(BF16)
        to_high_ref[1, :, at] = dot(ws[1][2 * PAIR :], grad[PAIR:], NN).astype(BF16)
        dq = dot(d_own, key, TN)
        dq_low = dot(ds[0][:PAIR], low_ref[0, :, at], TN)
        dq_high = dot(ds[1][2 * PAIR :], high_ref[0, :, at], TN)
        dq_ref[:PAIR, at] = ((dq[:PAIR] + dq_low) * FACTOR).astype(BF16)
        dq_ref[PAIR:, at] = ((dq[PAIR:] + dq_high) * FACTOR).astype(BF16)


def settle_kernel(own_ref, from_low_ref, from_high_ref, dk_ref, dv_ref):
    for i, out in enumerate((dk_ref, dv_ref)):
        out[:PAIR] = (own_ref[i, :PAIR] + from_low_ref[i].astype(F32)).astype(BF16)
        out[PAIR:] = (own_ref[i, PAIR:] + from_high_ref[i].astype(F32)).astype(BF16)


def shifted(shard, by):
    devices = lax.axis_size("ctx")
    pairs = [(i, i + by) for i in range(devices) if 0 <= i + by < devices]
    return lax.ppermute(shard, "ctx", pairs)


def copy_for_each(shard, axis):
    devices = lax.axis_size(axis)
    return lax.all_to_all(
        jnp.broadcast_to(shard[None], (devices, *shard.shape)), axis, 0, 0, tiled=True
    )


def shape(dims, dtype):
    return jax.ShapeDtypeStruct(dims, dtype)


def body(query_vecs, key_vecs, value_vecs, out_grad, block_mask, norm_gain):
    own_rows, features = query_vecs.shape
    heads = features // HEAD_FEATURES
    devices = lax.axis_size("ctx")
    to_next = jnp.stack([key_vecs[PAIR:], value_vecs[PAIR:]])
    to_previous = jnp.stack([key_vecs[:PAIR], value_vecs[:PAIR]])
    low = shifted(to_next, 1)
    high = shifted(to_previous, -1)
    mirror = lax.ppermute(block_mask, "ctx", [(i, devices - 1 - i) for i in range(devices)])
    mixed, rows, stats = pl.pallas_call(
        forward_kernel,
        out_shape=(
            shape((own_rows, features), F32),
            shape((heads, 2, 3, TILE, PAIR), F32),
            shape((2, own_rows), F32),
        ),
        in_specs=[SM, SM] + [VM] * 7,
        out_specs=(VM, VM, VM),
        scratch_shapes=[
            pltpu.VMEM((2, 2, TILE, 1, PAIR), F32),
            pltpu.VMEM((own_rows, HEAD_FEATURES), F32),
            pltpu.VMEM((own_rows, HEAD_FEATURES), F32),
        ],
        name="forward",
    )(block_mask, mirror, query_vecs, key_vecs, value_vecs, low, high, out_grad, norm_gain)
    all_stats = copy_for_each(stats, "head")
    normed, query_grad, own, to_low, to_high, gain_part = pl.pallas_call(
        backward_kernel,
        out_shape=(
            shape((own_rows, features), BF16),
            shape((own_rows, features), BF16),
            shape((2, own_rows, features), F32),
            shape((2, PAIR, features), BF16),
            shape((2, PAIR, features), BF16),
            shape((heads, HEAD_FEATURES), F32),
        ),
        in_specs=[VM] * 10,
        out_specs=(VM,) * 6,
        scratch_shapes=[pltpu.VMEM((own_rows, HEAD_FEATURES), F32)] * 2,
        name="backward",
    )(
        all_stats, query_vecs, key_vecs, value_vecs, low, high, out_grad, norm_gain, mixed, rows
    )
    from_high = shifted(to_low, -1)
    from_low = shifted(to_high, 1)
    gain_grad = copy_for_each(gain_part, "ctx").sum(axis=0) / math.sqrt(own_rows * devices)
    key_grad, value_grad = pl.pallas_call(
        settle_kernel,
        out_shape=(shape((own_rows, features), BF16),) * 2,
        in_specs=[VM] * 3,
        out_specs=(VM,) * 2,
        name="settle",
    )(own, from_low, from_high)
    return (normed, query_grad, key_grad, value_grad, gain_grad)


def solution(mesh):
    return jax.shard_map(
        body,
        mesh=mesh,
        in_specs=(
            P("ctx", "head"),
            P("ctx", "head"),
            P("ctx", "head"),
            P("ctx", "head"),
            P("ctx", None),
            P("head", None),
        ),
        out_specs=(
            P("ctx", "head"),
            P("ctx", "head"),
            P("ctx", "head"),
            P("ctx", "head"),
            P("head", None),
        ),
        check_vma=False,
    )
```

time: 176 us -> 82.3 us (0.47)
  local copies, waits for them, and re-layouts: 60.4 us -> 5.74 us
  matrix products: 23.3 us -> 0 us
  Pallas kernels: 0 us -> 19.9 us
  starting transfers between devices: 43.6 us -> 24.2 us
  other arithmetic: 19.1 us -> 0.77 us
  blocking collectives: 0 us -> 16.1 us
  waiting for transfers between devices: 27.1 us -> 13.5 us
    dot_general x14 -> x0, matrix products: 23.3 us -> none  [the longest x2 6.03 us: attend_backward(): jnp.einsum('bqhd,bkhd->bhqk', gradient_block_list, value_row_vectors, pre...]
    all_to_all x4 -> x1, starting transfers between devices: 27.5 us -> 6.98 us  [copy_for_each(): lax.all_to_all(jnp.broadcast_to(shard[None], (devices, *shard.shape)), ax...]
    pallas_call x0 -> x3, Pallas kernels: none -> 19.9 us  [the longest x1 9.42 us: body(): pl.pallas_call(backward_kernel, out_shape=(shape((own_rows, features), BF...]
    all_to_all x0 -> x1, blocking collectives: none -> 16.1 us  [copy_for_each(): lax.all_to_all(jnp.broadcast_to(shard[None], (devices, *shard.shape)), ax...]
    all_to_all x4 -> x1, waiting for transfers between devices: 12.3 us -> 0.01 us  [copy_for_each(): lax.all_to_all(jnp.broadcast_to(shard[None], (devices, *shard.shape)), ax...]
    another operation x4 -> x1, local copies, waits for them, and re-layouts: 12.5 us -> 1.26 us  [body(): to_previous = jnp.stack([key_vecs[:PAIR], value_vecs[:PAIR]])]
    unnamed x55 -> x12, local copies, waits for them, and re-layouts: 12.1 us -> 2.39 us
    transpose x2 -> x0, local copies, waits for them, and re-layouts: 8.65 us -> none  [attend_backward(): jnp.einsum('bhqk,bqhd->bkhd', rounded_values, gradient_block_list, prefer...]
  transfers between devices with their start and end apart: 8 -> 6, of which waited for: 5 -> 3; matrix products, arithmetic and copies ran while one was open for 40% -> 1% of each run, Pallas kernels for 0% -> 0%
where the time goes in v1:
time: 82.3 us; the launch traced here: 81 us
  starting transfers between devices  24.2 us (29%)
  Pallas kernels  19.9 us (24%)
  blocking collectives  16.1 us (20%)
  waiting for transfers between devices  13.5 us (16%)
  local copies, waits for them, and re-layouts  5.74 us (7%)
    ppermute x4, starting transfers between devices, shifted(): return lax.ppermute(shard, 'ctx', pairs)  17.1 us
    all_to_all x1, blocking collectives, copy_for_each(): lax.all_to_all(jnp.broadcast_to(shard[None], (devices, *shard.shape)), ax...  16.1 us
    pallas_call x1, Pallas kernels, body(): pl.pallas_call(backward_kernel, out_shape=(shape((own_rows, features), BF...  9.42 us
    pallas_call x1, Pallas kernels, body(): pl.pallas_call(forward_kernel, out_shape=(shape((own_rows, features), F32...  7.59 us
    ppermute x1, waiting for transfers between devices, body(): lax.ppermute(block_mask, 'ctx', [(i, devices - 1 - i) for i in range(devi...  7.22 us
    all_to_all x1, starting transfers between devices, copy_for_each(): lax.all_to_all(jnp.broadcast_to(shard[None], (devices, *shard.shape)), ax...  6.98 us
    ppermute x4, waiting for transfers between devices, shifted(): return lax.ppermute(shard, 'ctx', pairs)  6.32 us
    pallas_call x1, Pallas kernels, body(): pl.pallas_call(settle_kernel, out_shape=(shape((own_rows, features), BF16...  2.88 us
  transfers between devices with their start and end apart: 6, of which 3 were waited for; matrix products, arithmetic and copies ran while one was open for 1% of the time, Pallas kernels for 0%

profile of v1, /device:TPU:6, one launch (start us, length us, event | category | flops | bytes accessed | tf_op | source)
XLA Modules:
  0.0 81.0 jit_solution(1322671810010723923)
XLA Ops:
  0.6 1.3 %slice_bitcast_fusion = (bf16[1,128,1024]{2,1,0:T(8,128)(2,1)S(1)}, bf16[1,128,1024]{2,1,0:T(8,128)(2,1)S(1)}, bf16[1,128,1024]{2,1,0:T(8,128)(2,1)S(1)}, bf16[1,128,1024]{2,1,0:T(8,128)(2,1)S(1)}) fusion(bf16[256,1024]{1,0:T(8,128)(2,1)} %v_ref.3, bf16[256,1024]{1,0:T(8,128)(2,1)} %k_ref.3), kind=kLoop, calls=%fused_computation.2 | loop fusion | bytes 2097152 | tf_op jit(solution)/shard_map/stack | solution.py:223
  1.9 0.1 pad_maximum_fusion
  2.0 1.9 %collective-permute-start.1 = (bf16[2,128,1024]{2,1,0:T(8,128)(2,1)S(1)}, bf16[2,128,1024]{2,1,0:T(8,128)(2,1)S(1)}, u32[]{:S(2)}, u32[]{:S(2)}) collective-permute-start(bf16[2,128,1024]{2,1,0:T(8,128)(2,1)S(1)} %pad_maximum_fusion), channel_id=1, source_target_pairs={{0,4},{4,8},{8,12},{12,16},{16,20},{20,24},{24,28},{28,32},{32,36}... | collective-permute-start | bytes 1572872 | tf_op jit(solution)/shard_map/ppermute | solution.py:204
  3.9 0.1 pad_maximum_fusion.1
  4.0 6.7 %collective-permute-start.2 = (bf16[2,128,1024]{2,1,0:T(8,128)(2,1)S(1)}, bf16[2,128,1024]{2,1,0:T(8,128)(2,1)S(1)}, u32[]{:S(2)}, u32[]{:S(2)}) collective-permute-start(bf16[2,128,1024]{2,1,0:T(8,128)(2,1)S(1)} %pad_maximum_fusion.1), channel_id=1, source_target_pairs={{4,0},{8,4},{12,8},{16,12},{20,16},{24,20},{28,24},{32,28},{36,32}... | collective-permute-start | bytes 1572872 | tf_op jit(solution)/shard_map/ppermute | solution.py:204
  10.6 0.1 collective-permute-start
  10.7 7.2 %collective-permute-done.mirror_ref = s32[4,4]{1,0:T(4,128)S(1)} collective-permute-done((s32[4,4]{1,0:T(4,128)S(1)}, s32[4,4]{1,0:T(4,128)S(1)}, u32[]{:S(2)}, u32[]{:S(2)}) %collective-permute-start) | collective-permute-done | bytes 96 | tf_op jit(solution)/shard_map/ppermute | solution.py:226
  18.0 0.6 copy-done.5
  18.5 0.2 copy-done
  18.7 0.8 copy-done.1
  19.5 7.6 %forward.1 = (f32[256,1024]{1,0:T(8,128)}, f32[8,2,3,6,128]{4,3,2,1,0:T(8,128)}, f32[2,256]{1,0:T(2,128)}) custom-call(s32[4,4]{1,0:T(4,128)} %mask_ref.1, s32[4,4]{1,0:T(4,128)} %copy-done.5, bf16[256,1024]{1,0:T(8,128)(2,1)} %q_ref.3, bf16[256,1024]{1,0:T(8,128)(2,1)} %k_ref.3, bf16[256,1024]{1,0:T(8,128)(2,1)} %v_ref.3, bf16[2,128,1024]{2,1,0:T(8,128)(2,1)} %copy-done, ...), custom_call_target="tpu_custom_call" | custom-call | tf_op jit(solution)/shard_map/forward/pallas_call | solution.py:227
  27.1 0.7 broadcast_in_dim.4
  27.8 16.1 %all_to_all.10.stats_ref = f32[4,2,256]{2,1,0:T(2,128)} all-to-all(f32[4,2,256]{2,1,0:T(2,128)S(1)} %broadcast_in_dim.4), channel_id=1, replica_groups=mesh['ctx'=64,'head'=4] {'head'}, dimensions={0} | all-to-all | bytes 16384 | tf_op jit(solution)/shard_map/all_to_all | solution.py:209
  43.9 9.4 %backward.1 = (bf16[256,1024]{1,0:T(8,128)(2,1)}, bf16[256,1024]{1,0:T(8,128)(2,1)}, f32[2,256,1024]{2,1,0:T(8,128)}, bf16[2,128,1024]{2,1,0:T(8,128)(2,1)}, bf1...) custom-call(f32[4,2,256]{2,1,0:T(2,128)} %all_to_all.10.stats_ref, bf16[256,1024]{1,0:T(8,128)(2,1)} %q_ref.3, ...), custom_call_target="tpu_custom_call" | custom-call | tf_op jit(solution)/shard_map/backward/pallas_call | solution.py:244
  53.3 1.4 %broadcast_in_dim.5 = f32[64,8,128]{2,1,0:T(8,128)} broadcast(f32[8,128]{1,0:T(8,128)} %get-tuple-element.26), dimensions={1,2} | broadcast | bytes 266240 | tf_op jit(solution)/shard_map/broadcast_in_dim | solution.py:210
  54.7 7.0 %all-to-all-start.1 = ((f32[64,8,128]{2,1,0:T(8,128)}), f32[64,8,128]{2,1,0:T(8,128)S(1)}, u32[]{:S(2)}, u32[]{:S(2)}) async-start(f32[64,8,128]{2,1,0:T(8,128)} %broadcast_in_dim.5), calls=%async_computation.1 | async-start | bytes 524288 | tf_op jit(solution)/shard_map/all_to_all | solution.py:209
  61.7 2.0 %collective-permute-start.3 = (bf16[2,128,1024]{2,1,0:T(8,128)(2,1)}, bf16[2,128,1024]{2,1,0:T(8,128)(2,1)S(1)}, u32[]{:S(2)}, u32[]{:S(2)}) collective-permute-start(bf16[2,128,1024]{2,1,0:T(8,128)(2,1)} %get-tuple-element.22), channel_id=1, source_target_pairs={{0,4},{4,8},{8,12},{12,16},{16,20},{20,24},{24,28},{28,32},{32,36}... | collective-permute-start | bytes 1572872 | tf_op jit(solution)/shard_map/ppermute | solution.py:204
  63.7 6.5 %collective-permute-start.4 = (bf16[2,128,1024]{2,1,0:T(8,128)(2,1)}, bf16[2,128,1024]{2,1,0:T(8,128)(2,1)S(1)}, u32[]{:S(2)}, u32[]{:S(2)}) collective-permute-start(bf16[2,128,1024]{2,1,0:T(8,128)(2,1)} %get-tuple-element.23), channel_id=1, source_target_pairs={{4,0},{8,4},{12,8},{16,12},{20,16},{24,20},{28,24},{32,28},{36,32}... | collective-permute-start | bytes 1572872 | tf_op jit(solution)/shard_map/ppermute | solution.py:204
  70.3 0.1 reduce_sum.9
  70.4 0.6 broadcast_multiply_fusion
  71.0 4.5 %collective-permute-done.3.from_low_ref = bf16[2,128,1024]{2,1,0:T(8,128)(2,1)S(1)} collective-permute-done((bf16[2,128,1024]{2,1,0:T(8,128)(2,1)}, bf16[2,128,1024]{2,1,0:T(8,128)(2,1)S(1)}, u32[]{:S(2)}, u32[]{:S(2)}) %collective-permute-start.3) | collective-permute-done | bytes 524320 | tf_op jit(solution)/shard_map/ppermute | solution.py:204
  75.4 1.9 %collective-permute-done.4.from_high_ref = bf16[2,128,1024]{2,1,0:T(8,128)(2,1)S(1)} collective-permute-done((bf16[2,128,1024]{2,1,0:T(8,128)(2,1)}, bf16[2,128,1024]{2,1,0:T(8,128)(2,1)S(1)}, u32[]{:S(2)}, u32[]{:S(2)}) %collective-permute-start.4) | collective-permute-done | bytes 524320 | tf_op jit(solution)/shard_map/ppermute | solution.py:204
  77.3 0.8 copy-done.3
  78.1 2.9 %settle.1 = (bf16[256,1024]{1,0:T(8,128)(2,1)}, bf16[256,1024]{1,0:T(8,128)(2,1)}) custom-call(f32[2,256,1024]{2,1,0:T(8,128)} %get-tuple-element.21.own_ref, bf16[2,128,1024]{2,1,0:T(8,128)(2,1)} %copy-done.2, bf16[2,128,1024]{2,1,0:T(8,128)(2,1)} %copy-done.3), custom_call_target="tpu_custom_call" | custom-call | tf_op jit(solution)/shard_map/settle/pallas_call | solution.py:264
  (11 shorter events, 0.0 us)
Async XLA Ops:
  0.6 10.0 %copy-start.4 = (s32[4,4]{1,0:T(4,128)S(1)}, s32[4,4]{1,0:T(4,128)}, u32[]{:S(2)}) copy-start(s32[4,4]{1,0:T(4,128)} %mask_ref.1) | copy-start | bytes 196
  2.0 16.0 %collective-permute-start.1 = (bf16[2,128,1024]{2,1,0:T(8,128)(2,1)S(1)}, bf16[2,128,1024]{2,1,0:T(8,128)(2,1)S(1)}, u32[]{:S(2)}, u32[]{:S(2)}) collective-permute-start(bf16[2,128,1024]{2,1,0:T(8,128)(2,1)S(1)} %pad_maximum_fusion), channel_id=1, source_target_pairs={{0,4},{4,8},{8,12},{12,16},{16,20},{20,24},{24,28},{28,32},{32,36}... | collective-permute-start | bytes 1572872 | tf_op jit(solution)/shard_map/ppermute | solution.py:204
  4.0 14.0 %collective-permute-start.2 = (bf16[2,128,1024]{2,1,0:T(8,128)(2,1)S(1)}, bf16[2,128,1024]{2,1,0:T(8,128)(2,1)S(1)}, u32[]{:S(2)}, u32[]{:S(2)}) collective-permute-start(bf16[2,128,1024]{2,1,0:T(8,128)(2,1)S(1)} %pad_maximum_fusion.1), channel_id=1, source_target_pairs={{4,0},{8,4},{12,8},{16,12},{20,16},{24,20},{28,24},{32,28},{36,32}... | collective-permute-start | bytes 1572872 | tf_op jit(solution)/shard_map/ppermute | solution.py:204
  10.6 7.3 %collective-permute-start = (s32[4,4]{1,0:T(4,128)S(1)}, s32[4,4]{1,0:T(4,128)S(1)}, u32[]{:S(2)}, u32[]{:S(2)}) collective-permute-start(s32[4,4]{1,0:T(4,128)S(1)} %copy-done.4), channel_id=1, source_target_pairs={{0,252},{4,248},{8,244},{12,240},{16,236},{20,232},{24,228},{28,22... | collective-permute-start | bytes 200 | tf_op jit(solution)/shard_map/ppermute | solution.py:226
  17.9 0.6 copy-start.5
  17.9 0.8 copy-start
  18.7 0.8 copy-start.1
  54.7 15.6 %all-to-all-start.1 = ((f32[64,8,128]{2,1,0:T(8,128)}), f32[64,8,128]{2,1,0:T(8,128)S(1)}, u32[]{:S(2)}, u32[]{:S(2)}) async-start(f32[64,8,128]{2,1,0:T(8,128)} %broadcast_in_dim.5), calls=%async_computation.1 | async-start | bytes 524288 | tf_op jit(solution)/shard_map/all_to_all | solution.py:209
  61.7 13.7 %collective-permute-start.3 = (bf16[2,128,1024]{2,1,0:T(8,128)(2,1)}, bf16[2,128,1024]{2,1,0:T(8,128)(2,1)S(1)}, u32[]{:S(2)}, u32[]{:S(2)}) collective-permute-start(bf16[2,128,1024]{2,1,0:T(8,128)(2,1)} %get-tuple-element.22), channel_id=1, source_target_pairs={{0,4},{4,8},{8,12},{12,16},{16,20},{20,24},{24,28},{28,32},{32,36}... | collective-permute-start | bytes 1572872 | tf_op jit(solution)/shard_map/ppermute | solution.py:204
  63.7 13.5 %collective-permute-start.4 = (bf16[2,128,1024]{2,1,0:T(8,128)(2,1)}, bf16[2,128,1024]{2,1,0:T(8,128)(2,1)S(1)}, u32[]{:S(2)}, u32[]{:S(2)}) collective-permute-start(bf16[2,128,1024]{2,1,0:T(8,128)(2,1)} %get-tuple-element.23), channel_id=1, source_target_pairs={{4,0},{8,4},{12,8},{16,12},{20,16},{24,20},{28,24},{32,28},{36,32}... | collective-permute-start | bytes 1572872 | tf_op jit(solution)/shard_map/ppermute | solution.py:204
  75.4 1.9 %copy-start.2 = (bf16[2,128,1024]{2,1,0:T(8,128)(2,1)}, bf16[2,128,1024]{2,1,0:T(8,128)(2,1)S(1)}, u32[]{:S(2)}) copy-start(bf16[2,128,1024]{2,1,0:T(8,128)(2,1)S(1)} %collective-permute-done.3.from_low_ref) | copy-start | bytes 1572868
  77.3 0.8 copy-start.3
